TPU v7x, 32 devices: a whole 2x2x4 slice. The times are simulated.
32 devices in a mesh: tm: 4 (over z), tmpl: 8 (over y, x, core).
Axes of the slice: x: 2, y: 2, z: 4, core: 2. Of those that a mesh axis runs over, the one named last changes fastest.
Arguments:
- strain: float32 [8, 131072], P('tmpl', 'tm'), may hold values from -6 to 6
- psd_bins: int32 [4, 65536], P(None, 'tmpl'), may hold values from 0 to 8191, as said below
- psd_values: float32 [4, 8192], P('tm'), may hold values from 0.25 to 4
- chirp_slope: int32 [16], P('tmpl'), may hold values from 0 to 1023
- chirp_curve: int32 [16], P('tmpl'), may hold values from 1 to 63
Outputs:
- snr: float32 [16, 1048576], P('tmpl', 'tm')
Inputs may be any that keep to these rules, and one draw needn't show every extreme that they name: psd_bins[r, c] names the row of psd_values that serves frequency bin r * 65536 + c.
All inputs are finite; a program needn't handle non-finite values.
Results may differ from a plain program's by a relative error of at most 0.0003.
Values sent between devices are 32-bit elements; how exact they have to be, the bound alone decides.
A program may use at most 128 MiB of HBM per device.

v0:
```python
import math

import jax
import jax.numpy as jnp
from jax import lax
from jax.sharding import PartitionSpec as P

OR = 32768


HIGHEST = lax.Precision.HIGHEST
TWO_PI = 2.0 * math.pi


def shifted(block, axis, distance):
    devices = range(lax.axis_size(axis))
    route = [(i - distance, i) for i in devices if i - distance in devices]
    return lax.ppermute(block, axis, route)


def split_sizes(length):
    count = 0
    while length > 512:
        length = length // 128
        count = count + 1
    return [length] + [128] * count


def angle_table(rows_count, cols_count, modulus, direction):
    product = (
        jnp.arange(rows_count, dtype=jnp.int32)[:, None]
        * jnp.arange(cols_count, dtype=jnp.int32)[None, :]
    )
    angles = (product % modulus).astype(jnp.float32) * (direction * TWO_PI / modulus)
    return (jnp.cos(angles), jnp.sin(angles))


def complex_left(cos_part, sin_part, real_part, imag_part):
    new_re = jnp.einsum("qp,...pk->...qk", cos_part, real_part, precision=HIGHEST) - jnp.einsum(
        "qp,...pk->...qk", sin_part, imag_part, precision=HIGHEST
    )
    new_im = jnp.einsum("qp,...pk->...qk", sin_part, real_part, precision=HIGHEST) + jnp.einsum(
        "qp,...pk->...qk", cos_part, imag_part, precision=HIGHEST
    )
    return (new_re, new_im)


def apply_sizes(real_part, imag_part, sizes, direction):
    length = real_part.shape[-1]
    if len(sizes) == 1:
        cos_part, sin_part = angle_table(length, length, length, direction)
        new_re = jnp.matmul(real_part, cos_part, precision=HIGHEST) - jnp.matmul(
            imag_part, sin_part, precision=HIGHEST
        )
        new_im = jnp.matmul(real_part, sin_part, precision=HIGHEST) + jnp.matmul(
            imag_part, cos_part, precision=HIGHEST
        )
        return (new_re, new_im)
    outer_size = sizes[0]
    inner_size = length // outer_size
    leading = real_part.shape[:-1]
    real_part = real_part.reshape(leading + (outer_size, inner_size))
    imag_part = imag_part.reshape(leading + (outer_size, inner_size))
    mat_cos, mat_sin = angle_table(outer_size, outer_size, outer_size, direction)
    real_part, imag_part = complex_left(mat_cos, mat_sin, real_part, imag_part)
    cos_part, sin_part = angle_table(outer_size, inner_size, length, direction)
    real_part, imag_part = (
        real_part * cos_part - imag_part * sin_part,
        real_part * sin_part + imag_part * cos_part,
    )
    return apply_sizes(real_part, imag_part, sizes[1:], direction)


def transform(real_part, imag_part, direction):
    length = real_part.shape[-1]
    leading = real_part.shape[:-1]
    sizes = split_sizes(length)
    new_re, new_im = apply_sizes(real_part, imag_part, sizes, direction)
    lead_count = len(leading)
    last_axis = new_re.ndim - 1
    order = tuple(range(lead_count)) + tuple(range(last_axis, lead_count - 1, -1))
    new_re = jnp.transpose(new_re, order)
    new_im = jnp.transpose(new_im, order)
    return (new_re.reshape(leading + (length,)), new_im.reshape(leading + (length,)))


def chirp_phase(frequency, slope, curve, modulus):
    high_part = frequency // 1024
    low_part = frequency % 1024
    square = 2 * high_part * low_part % (modulus // 1024) * 1024 + low_part * low_part
    square = square % modulus
    return (slope * frequency + curve * square) % modulus


def amplitude_of(frequency, k_low, k_cut):
    ratio = frequency.astype(jnp.float32) / k_low
    inside = (frequency >= k_low) & (frequency < k_cut)
    return jnp.where(inside, jnp.power(jnp.maximum(ratio, 1.0), -7.0 / 6.0), 0.0)


def template_parts(frequency, chirp_slope, chirp_curve, modulus, k_low, k_cut):
    phase = chirp_phase(frequency[None, :], chirp_slope[:, None], chirp_curve[:, None], modulus)
    angles = phase.astype(jnp.float32) * (TWO_PI / modulus)
    amplitude = amplitude_of(frequency, k_low, k_cut)
    return (amplitude * jnp.cos(angles), -amplitude * jnp.sin(angles))


def local(strain, psd_bins, psd_values, chirp_slope, chirp_curve):
    groups = lax.axis_size("tmpl")
    member = lax.axis_index("tmpl")
    own_part = strain[0]
    edge_tail = shifted(own_part, "tm", 1)
    local_seq = jnp.concatenate([edge_tail, own_part])
    sub_len = local_seq.shape[0]
    total_len = sub_len * groups
    block_len = sub_len // groups
    norm_scale = 1.0 / math.sqrt(total_len)
    k_low = total_len // 200
    k_cut = 3 * total_len // 8
    band_rows = 3 * groups // 8
    inv_psd = 1.0 / jnp.take(psd_values[0], psd_bins[:band_rows])
    local_re, local_im = transform(local_seq, jnp.zeros_like(local_seq), -1.0)
    index_k = jnp.arange(sub_len, dtype=jnp.int32)
    angles = (member * index_k % total_len).astype(jnp.float32) * (-TWO_PI / total_len)
    twist_cos = jnp.cos(angles)
    twist_sin = jnp.sin(angles)
    part_re = local_re * twist_cos - local_im * twist_sin
    part_im = local_re * twist_sin + local_im * twist_cos
    cross_cos, cross_sin = angle_table(band_rows, groups, groups, -1.0)
    piece_re = lax.all_to_all(
        part_re.reshape(groups, 1, block_len), "tmpl", split_axis=0, concat_axis=1, tiled=True
    )
    piece_im = lax.all_to_all(
        part_im.reshape(groups, 1, block_len), "tmpl", split_axis=0, concat_axis=1, tiled=True
    )
    spec_re, spec_im = complex_left(cross_cos, cross_sin, piece_re[0], piece_im[0])
    white_re = spec_re * inv_psd * norm_scale
    white_im = spec_im * inv_psd * norm_scale
    white_re, white_im, inv_whole = (
        lax.all_gather(white_re, "tmpl", axis=1, tiled=True),
        lax.all_gather(white_im, "tmpl", axis=1, tiled=True),
        lax.all_gather(inv_psd, "tmpl", axis=1, tiled=True),
    )
    band_len = band_rows * sub_len
    white_re = white_re.reshape(band_len)
    white_im = white_im.reshape(band_len)
    frequency = jnp.arange(band_len, dtype=jnp.int32)
    tmpl_re, tmpl_im = template_parts(frequency, chirp_slope, chirp_curve, total_len, k_low, k_cut)
    inv_whole = inv_whole.reshape(band_len)
    sigma_sq = jnp.sum((tmpl_re * tmpl_re + tmpl_im * tmpl_im) * inv_whole, axis=-1)
    coef_re = white_re * tmpl_re + white_im * tmpl_im
    coef_im = white_im * tmpl_re - white_re * tmpl_im
    widths = ((0, 0), (0, total_len - band_len))
    series_re, series_im = transform(jnp.pad(coef_re, widths), jnp.pad(coef_im, widths), 1.0)
    magnitude = (
        jnp.sqrt(series_re * series_re + series_im * series_im) / jnp.sqrt(sigma_sq)[..., None]
    )
    return magnitude[:, OR * groups :]


def solution(mesh):
    placed = (P("tmpl", "tm"), P(None, "tmpl"), P("tm", None), P("tmpl"), P("tmpl"))
    return jax.shard_map(
        local, mesh=mesh, in_specs=placed, out_specs=P("tmpl", "tm"), check_vma=False
    )
```

profile of v0, /device:TPU:9, one launch (start us, length us, event | category | flops | bytes accessed | tf_op | source)
XLA Modules:
  0.0 430.7 jit_solution(9449449563915326860)
XLA Ops:
  3.3 5.9 %fusion.81 = f32[512,128]{1,0:T(8,128)} fusion(), kind=kOutput, calls=%fused_computation.114 | convolution fusion | flops 406323200 | bytes 262144 | tf_op jit(solution)/shard_map/qp,...pk->...qk/dot_general | solution.py:39
  12.6 9.1 %fusion.55 = (f32[32,16384]{1,0:T(8,128)S(1)}, f32[32,16384]{1,0:T(8,128)}) fusion(), kind=kLoop, calls=%fused_computation.91 | loop fusion | flops 7340032 | bytes 4194304 | tf_op jit(solution)/shard_map/sin | solution.py:35
  21.8 135.5 %gather_fusion = f32[24576]{0:T(1024)S(1)} fusion(f32[8192]{0:T(1024)S(1)} %bitcast.120, s32[24576]{0:T(1024)S(1)} %broadcast_clamp_fusion), kind=kCustom, calls=%fused_computation | custom fusion | bytes 294912 | tf_op jit(solution)/shard_map/jit(_take)/gather | solution.py:121
  175.6 14.9 %fusion.127 = f32[128,512]{1,0:T(8,128)} fusion(f32[512,128]{1,0:T(8,128)S(1)} %convolution_add_fusion.3, f32[512,128]{1,0:T(8,128)S(1)} %convolution_subtract_fusion.3), kind=kOutput, calls=%fused_computation.182 | convolution fusion | flops 102006784 | bytes 786432 | tf_op jit(solution)/shard_map/dot_general | solution.py:52
  203.0 12.8 %all_gather.11 = f32[3,65536]{1,0:T(4,128)S(1)} all-gather(f32[3,8192]{1,0:T(4,128)S(1)} %select_divide_fusion), channel_id=1, replica_groups=mesh['tm'=4,'tmpl'=8] {'tmpl'}, dimensions={1}, use_global_device_ids=true | all-gather | bytes 884736 | tf_op jit(solution)/shard_map/all_gather | solution.py:142
  229.6 11.1 %all_gather.10 = f32[3,65536]{1,0:T(4,128)S(1)} all-gather(f32[3,8192]{1,0:T(4,128)S(1)} %fusion.3), channel_id=1, replica_groups=mesh['tm'=4,'tmpl'=8] {'tmpl'}, dimensions={1}, use_global_device_ids=true | all-gather | bytes 884736 | tf_op jit(solution)/shard_map/all_gather | solution.py:141
  245.1 11.2 %all_gather.9 = f32[3,65536]{1,0:T(4,128)S(1)} all-gather(f32[3,8192]{1,0:T(4,128)S(1)} %fusion.5), channel_id=1, replica_groups=mesh['tm'=4,'tmpl'=8] {'tmpl'}, dimensions={1}, use_global_device_ids=true | all-gather | bytes 884736 | tf_op jit(solution)/shard_map/all_gather | solution.py:140
  257.8 30.0 %multiply_subtract_fusion.1 = (f32[2,196608]{1,0:T(2,128)S(1)}, f32[2,196608]{1,0:T(2,128)S(1)}, f32[2]{0:T(128)S(1)}) fusion(f32[196608]{0:T(1024)} %mul.763, f32[196608]{0:T(1024)} %mul.743, s32[196608]{0:T(1024)} %add_select_fusion.2, s32[2]{0:T(128)S(1)} %copy-done.5, s32[2]{0:T(128)S(1)} %copy-done.6, f32[196608]{0:T(1024)} %get-tuple-element.12, ...), kind=kLoop, calls=%fused_computation.57 | loop fusion | flops 11403262 | bytes 7864344 | tf_op jit(solution)/shard_map/sub | solution.py:152
  287.8 6.9 %pad.7 = f32[2,524288]{1,0:T(2,128)S(1)} pad(f32[2,196608]{1,0:T(2,128)S(1)} %get-tuple-element.8, f32[]{:T(128)} %constant.193.clone.1), padding=0_0x0_327680 | pad | bytes 5767172 | tf_op jit(solution)/shard_map/jit(_pad)/pad | solution.py:154
  294.7 6.6 %fusion.16 = f32[2,16384,32]{1,2,0:T(8,128)S(1)} fusion(f32[1,2,32,16384]{3,1,2,0:T(2,128)S(1)} %bitcast.125), kind=kOutput, calls=%fused_computation.21 | convolution fusion | flops 402667520 | bytes 8388608 | tf_op jit(solution)/shard_map/qp,...pk->...qk/dot_general | solution.py:42
  301.3 6.8 %fusion.18 = f32[2,16384,32]{1,2,0:T(8,128)S(1)} fusion(f32[1,2,32,16384]{3,1,2,0:T(2,128)S(1)} %bitcast.126), kind=kOutput, calls=%fused_computation.23 | convolution fusion | flops 402667520 | bytes 8388608 | tf_op jit(solution)/shard_map/qp,...pk->...qk/dot_general | solution.py:39
  308.1 6.5 %pad.8 = f32[2,524288]{1,0:T(2,128)S(1)} pad(f32[2,196608]{1,0:T(2,128)S(1)} %get-tuple-element.7, f32[]{:T(128)} %constant.193.clone.1), padding=0_0x0_327680 | pad | bytes 5767172 | tf_op jit(solution)/shard_map/jit(_pad)/pad | solution.py:154
  314.7 6.7 %fusion = f32[2,32,16384]{2,1,0:T(8,128)S(1)} fusion(f32[2,16384,32]{1,2,0:T(8,128)S(1)} %fusion.18, f32[1,2,32,16384]{3,1,2,0:T(2,128)S(1)} %bitcast.121), kind=kOutput, calls=%fused_computation.3 | convolution fusion | flops 403716096 | bytes 12582912 | tf_op jit(solution)/shard_map/qp,...pk->...qk/dot_general | solution.py:39
  321.4 8.5 %multiply_subtract_fusion = (f32[2,32,16384]{2,1,0:T(8,128)}, f32[2,32,16384]{2,1,0:T(8,128)S(1)}) fusion(f32[2,32,16384]{2,1,0:T(8,128)S(1)} %fusion, f32[32,16384]{1,0:T(8,128)S(1)} %get-tuple-element.14, f32[32,16384]{1,0:T(8,128)S(1)} %copy-done.2, f32[2,16384,32]{1,2,0:T(8,128)S(1)} %fusion.16, f32[1,2,32,16384]{3,1,2,0:T(2,128)S(1)} %bitcast.122), kind=kOutput, calls=%fused_computation.33 | convolution fusion | flops 410007552 | bytes 25165824 | tf_op jit(solution)/shard_map/qp,...pk->...qk/dot_general | solution.py:42
  333.6 7.7 %fusion.8 = f32[2,32,128,128]{3,2,1,0:T(8,128)S(1)} fusion(f32[2,32,128,128]{3,2,1,0:T(8,128)S(1)} %bitcast.127), kind=kOutput, calls=%fused_computation.13 | convolution fusion | flops 1610842112 | bytes 8388608 | tf_op jit(solution)/shard_map/qp,...pk->...qk/dot_general | solution.py:39
  341.2 8.0 %fusion.6 = f32[2,32,128,128]{3,2,1,0:T(8,128)S(1)} fusion(f32[2,32,128,128]{3,2,1,0:T(8,128)S(1)} %bitcast.128), kind=kOutput, calls=%fused_computation.11 | convolution fusion | flops 1610842112 | bytes 8388608 | tf_op jit(solution)/shard_map/qp,...pk->...qk/dot_general | solution.py:42
  349.3 7.8 %fusion.26 = f32[2,32,128,128]{3,2,1,0:T(8,128)S(1)} fusion(f32[2,32,128,128]{3,2,1,0:T(8,128)S(1)} %fusion.8, f32[2,32,128,128]{3,2,1,0:T(8,128)S(1)} %bitcast.123), kind=kOutput, calls=%fused_computation.44 | convolution fusion | flops 1611890688 | bytes 12582912 | tf_op jit(solution)/shard_map/qp,...pk->...qk/dot_general | solution.py:39
  357.1 8.0 %fusion.29 = f32[2,32,128,128]{3,2,1,0:T(8,128)S(1)} fusion(f32[2,32,128,128]{3,2,1,0:T(8,128)S(1)} %fusion.6, f32[2,32,128,128]{3,2,1,0:T(8,128)S(1)} %bitcast.124), kind=kOutput, calls=%fused_computation.45 | convolution fusion | flops 1611890688 | bytes 12582912 | tf_op jit(solution)/shard_map/qp,...pk->...qk/dot_general | solution.py:42
  365.0 7.2 %fusion.48 = f32[2,32,128,128]{3,2,1,0:T(8,128)S(1)} fusion(f32[2,32,128,128]{3,2,1,0:T(8,128)S(1)} %fusion.29, f32[2,32,128,128]{3,2,1,0:T(8,128)S(1)} %fusion.26, f32[128,128]{0,1:T(8,128)S(1)} %copy.49, f32[128,128]{0,1:T(8,128)S(1)} %copy.46), kind=kOutput, calls=%fused_computation.75 | convolution fusion | flops 1613987840 | bytes 12713984 | tf_op jit(solution)/shard_map/dot_general | solution.py:55
  372.3 7.4 %fusion.46 = f32[2,32,128,128]{3,2,1,0:T(8,128)S(1)} fusion(f32[2,32,128,128]{3,2,1,0:T(8,128)S(1)} %fusion.29, f32[2,32,128,128]{3,2,1,0:T(8,128)S(1)} %fusion.26, f32[128,128]{0,1:T(8,128)S(1)} %copy.49, f32[128,128]{0,1:T(8,128)S(1)} %copy.46), kind=kOutput, calls=%fused_computation.74 | convolution fusion | flops 1613987840 | bytes 12713984 | tf_op jit(solution)/shard_map/dot_general | solution.py:52
  379.7 7.1 %fusion.50 = f32[2,32,128,128]{3,2,1,0:T(8,128)S(1)} fusion(f32[2,32,128,128]{3,2,1,0:T(8,128)S(1)} %fusion.29, f32[2,32,128,128]{3,2,1,0:T(8,128)S(1)} %fusion.26, f32[128,128]{0,1:T(8,128)S(1)} %copy.49, f32[128,128]{0,1:T(8,128)S(1)} %copy.46), kind=kOutput, calls=%fused_computation.76 | convolution fusion | flops 1613987840 | bytes 12713984 | tf_op jit(solution)/shard_map/dot_general | solution.py:52
  386.8 9.8 %sqrt_bitcast_fusion = f32[2,128,128,32]{1,2,3,0:T(8,128)} fusion(f32[2,32,128,128]{3,2,1,0:T(8,128)S(1)} %fusion.48, f32[2,32,128,128]{3,2,1,0:T(8,128)S(1)} %fusion.50, f32[2,32,128,128]{3,2,1,0:T(8,128)S(1)} %fusion.46, f32[2,32,128,128]{3,2,1,0:T(8,128)S(1)} %fusion.29, f32[2,32,128,128]{3,2,1,0:T(8,128)S(1)} %fusion.26, f32[128,128]{0,1:T(8,128)S(1)} %copy.49, ...), kind=kOutput, calls=%fused_computation.31 | convolution fusion | flops 1619230720 | bytes 25296896 | tf_op jit(solution)/shard_map/dot_general | solution.py:55
  396.7 14.8 %copy.54 = f32[2,128,128,32]{3,2,1,0:T(8,128)} copy(f32[2,128,128,32]{1,2,3,0:T(8,128)} %sqrt_bitcast_fusion) | data formatting | bytes 8388608 | tf_op jit(solution)/shard_map/sqrt | solution.py:156
  411.5 15.7 %sqrt.18 = f32[2,524288]{1,0:T(2,128)} reshape(f32[2,128,128,32]{3,2,1,0:T(8,128)} %copy.54) | data formatting | bytes 8388608 | tf_op jit(solution)/shard_map/sqrt | solution.py:156
  (57 shorter events, 63.8 us)
Async XLA Ops:
  0.0 21.8 %copy-start = (f32[1,8192]{1,0:T(1,128)S(1)}, f32[1,8192]{1,0:T(1,128)}, u32[]{:S(2)}) copy-start(f32[1,8192]{1,0:T(1,128)} %param.7) | copy-start | bytes 98308
  0.0 163.3 %collective-permute-start = (f32[32768]{0:T(1024)}, f32[32768]{0:T(1024)S(1)}, u32[]{:S(2)}, u32[]{:S(2)}) collective-permute-start(f32[32768]{0:T(1024)} %bitcast.131), channel_id=1, source_target_pairs={{0,8},{8,16},{16,24},{1,9},{9,17},{17,25},{2,10},{10,18},{18,26},{... | collective-permute-start | bytes 393224 | tf_op jit(solution)/shard_map/ppermute | solution.py:18
  9.2 12.4 %copy-start.4 = (s32[4,8192]{1,0:T(4,128)S(1)}, s32[4,8192]{1,0:T(4,128)}, u32[]{:S(2)}) copy-start(s32[4,8192]{1,0:T(4,128)} %param.6) | copy-start | bytes 393220
  157.3 6.0 %copy-start.7 = (f32[1,32768]{1,0:T(1,128)S(1)}, f32[1,32768]{1,0:T(1,128)}, u32[]{:S(2)}) copy-start(f32[1,32768]{1,0:T(1,128)} %param.5) | copy-start | bytes 393220
  173.9 16.6 %copy-start.8 = (f32[512,128]{1,0:T(8,128)}, f32[512,128]{1,0:T(8,128)S(1)}, u32[]{:S(2)}) copy-start(f32[512,128]{1,0:T(8,128)S(1)} %convolution_add_fusion.3) | copy-start | bytes 786436
  197.7 21.5 %all-to-all-start = ((f32[8,1,8192]{2,1,0:T(1,128)}), f32[8,1,8192]{2,1,0:T(1,128)}, u32[]{:S(2)}, u32[]{:S(2)}) async-start(f32[8,1,8192]{2,1,0:T(1,128)} %copy.42), calls=%async_computation | async-start | bytes 524288 | tf_op jit(solution)/shard_map/all_to_all | solution.py:130
  219.2 9.2 %all-to-all-start.1 = ((f32[8,1,8192]{2,1,0:T(1,128)}), f32[8,1,8192]{2,1,0:T(1,128)S(1)}, u32[]{:S(2)}, u32[]{:S(2)}) async-start(f32[8,1,8192]{2,1,0:T(1,128)} %copy.43), calls=%async_computation.1 | async-start | bytes 524288 | tf_op jit(solution)/shard_map/all_to_all | solution.py:133
  222.7 35.1 %copy-start.5 = (s32[2]{0:T(128)S(1)}, s32[2]{0:T(128)}, u32[]{:S(2)}) copy-start(s32[2]{0:T(128)} %param.9) | copy-start | bytes 28
  222.7 35.1 %copy-start.6 = (s32[2]{0:T(128)S(1)}, s32[2]{0:T(128)}, u32[]{:S(2)}) copy-start(s32[2]{0:T(128)} %param.8) | copy-start | bytes 28
  228.4 0.7 copy-start.3
  314.7 6.7 %copy-start.2 = (f32[32,16384]{1,0:T(8,128)S(1)}, f32[32,16384]{1,0:T(8,128)}, u32[]{:S(2)}) copy-start(f32[32,16384]{1,0:T(8,128)} %get-tuple-element.15) | copy-start | bytes 6291460
  411.5 18.8 %copy-start.1 = (f32[1,8192]{1,0:T(1,128)S(1)}, f32[1,8192]{1,0:T(1,128)}, u32[]{:S(2)}) copy-start(f32[1,8192]{1,0:T(1,128)} %param.7) | copy-start | bytes 98308
where the time goes:
time: 437 us; the launch traced here: 431 us
  local copies, waits for them, and re-layouts  192 us (44%)
  matrix products  139 us (32%)
  other arithmetic  47.9 us (11%)
  blocking collectives  35.1 us (8%)
  starting transfers between devices  11.7 us (3%)
    gather x2, local copies, waits for them, and re-layouts, local(): inv_psd = 1.0 / jnp.take(psd_values[0], psd_bins[:band_rows])  136 us
    sqrt x2, local copies, waits for them, and re-layouts, local(): jnp.sqrt(series_re * series_re + series_im * series_im)  30.5 us
    sub x1, other arithmetic, local(): coef_im = white_im * tmpl_re - white_re * tmpl_im  30 us
    dot_general x4, matrix products, complex_left(): jnp.einsum('qp,...pk->...qk', cos_part, imag_part, precision=HIGHEST)  22.6 us
    dot_general x2, matrix products, apply_sizes(): jnp.matmul(real_part, cos_part, precision=HIGHEST)  22 us
    dot_general x4, matrix products, complex_left(): jnp.einsum('qp,...pk->...qk', cos_part, real_part, precision=HIGHEST)  21.7 us
    dot_general x4, matrix products, complex_left(): jnp.einsum('qp,...pk->...qk', sin_part, imag_part, precision=HIGHEST)  21.7 us
    dot_general x4, matrix products, complex_left(): jnp.einsum('qp,...pk->...qk', sin_part, real_part, precision=HIGHEST)  20.8 us
  transfers between devices with their start and end apart: 3, of which 1 were waited for; matrix products, arithmetic and copies ran while one was open for 38% of the time, Pallas kernels for 0%

commit v1 on v0

v1 whole, which is shorter than its diff:
```python
import functools
import math

import jax
import jax.numpy as jnp
import numpy as np
from jax import lax
from jax.experimental import pallas as pl
from jax.experimental.pallas import tpu as pltpu
from jax.sharding import PartitionSpec as P

TWO_PI = 2.0 * math.pi
LANE = 128
FINE = 32
COARSE = 16
VMEM_LIMIT = 60 * 1024 * 1024
BF16 = jnp.bfloat16
F32 = jnp.float32
NN = (((1,), (0,)), ((), ()))
NT = (((1,), (1,)), ((), ()))


def shifted(block, axis, distance):
    devices = range(lax.axis_size(axis))
    route = [(i - distance, i) for i in devices if i - distance in devices]
    return lax.ppermute(block, axis, route)


def base_table(rows, cols, modulus, direction, start=0):
    first = start + FINE * np.arange(rows // FINE, dtype=np.int64)
    index = np.concatenate([first, np.arange(FINE, dtype=np.int64)])
    angle = (index[:, None] * np.asarray(cols, dtype=np.int64)[None, :] % modulus) * (
        direction * TWO_PI / modulus
    )
    return jnp.asarray(np.stack([np.cos(angle), np.sin(angle)]).astype(np.float32))


def product_rows(table, outer, coarse_count):
    c1 = table[0, pl.ds(outer, 1), :]
    s1 = table[1, pl.ds(outer, 1), :]
    c0 = table[0, coarse_count : coarse_count + FINE, :]
    s0 = table[1, coarse_count : coarse_count + FINE, :]
    return c1 * c0 - s1 * s0, s1 * c0 + c1 * s0


def halves(value):
    high = value.astype(BF16)
    return high, (value - high.astype(F32)).astype(BF16)


def put(ref, slot, index, value):
    high, low = halves(value)
    ref[(slot, 0) + index] = high
    ref[(slot, 1) + index] = low


def put_factor(ref, index, re, im):
    put(ref, 0, index, re)
    put(ref, 1, index, im - re)
    put(ref, 2, index, re + im)


def dot3(a, b, slot, dims):
    def one(i, j):
        return lax.dot_general(a[slot, i], b[slot, j], dims, preferred_element_type=F32)

    return one(0, 0) + (one(0, 1) + one(1, 0))


def complex_dot(a, b, dims):
    k1 = dot3(a, b, 0, dims)
    k2 = dot3(a, b, 1, dims)
    k3 = dot3(a, b, 2, dims)
    return k1 - k3, k1 + k2


def inverse_density(bins_ref, table_ref, out_ref):
    rows = bins_ref.shape[0]
    step = next(n for n in (64, 48, 32, 24, 16, 8) if rows % n == 0)
    for first in range(0, rows, step):
        bins = bins_ref[first : first + step, :]
        high = bins // LANE
        low = bins % LANE

        def body(row, total):
            line = jnp.broadcast_to(table_ref[pl.ds(row, 1), :], (step, LANE))
            return jnp.where(
                high == row,
                jnp.take_along_axis(line, low, axis=1, mode="promise_in_bounds"),
                total,
            )

        picked = lax.fori_loop(
            0, table_ref.shape[0], body, jnp.ones((step, LANE), F32), unroll=4
        )
        out_ref[first : first + step, :] = 1.0 / picked


def forward_kernel(
    block, segment_rows, member_rows, templates, scale,
    packed_ref, f1_ref, twist_ref, f2_ref, amp_ref, chirp_ref,
    re_ref, im_ref, sigma_ref,
    x_ref, f1_buf, y_buf, f2_buf, weight_ref,
):
    step = pl.program_id(0)
    groups = packed_ref.shape[0]
    depth = re_ref.shape[1]
    coarse2 = depth // FINE
    f1_coarse = f1_ref.shape[1] - FINE
    twist_coarse = twist_ref.shape[1] - FINE

    @pl.when(step == 0)
    def _():
        for j in range(groups):
            high, low = halves(packed_ref[j, :segment_rows, :])
            x_ref[0, :, j * LANE : (j + 1) * LANE] = high
            x_ref[1, :, j * LANE : (j + 1) * LANE] = low

        @pl.loop(0, coarse2)
        def _(outer):
            c, s = product_rows(f2_ref, outer, coarse2)
            put_factor(f2_buf, (pl.ds(pl.multiple_of(outer * FINE, FINE), FINE),), c, s)

        sigma_ref[...] = jnp.zeros_like(sigma_ref)

    per_block = block // FINE

    @pl.loop(0, per_block)
    def _(i):
        rows = (pl.ds(pl.multiple_of(i * FINE, FINE), FINE),)
        c, s = product_rows(f1_ref, step * per_block + i, f1_coarse)
        put(f1_buf, 0, rows, c)
        put(f1_buf, 1, rows, s)

    def real_dot(slot):
        def one(i, j):
            return lax.dot_general(f1_buf[slot, i], x_ref[j], NN, preferred_element_type=F32)

        return one(0, 0) + (one(0, 1) + one(1, 0))

    y_re = real_dot(0)
    y_im = real_dot(1)
    for i in range(per_block):
        span = slice(i * FINE, (i + 1) * FINE)
        c, s = product_rows(twist_ref, step * per_block + i, twist_coarse)
        a, b = y_re[span], y_im[span]
        re = a * c - b * s
        im = a * s + b * c
        put(y_buf, 0, (span,), re + im)
        put(y_buf, 1, (span,), re)
        put(y_buf, 2, (span,), im)
    x_re, x_im = complex_dot(f2_buf, y_buf, NT)

    bands = (packed_ref.shape[1] - segment_rows) // member_rows // (re_ref.shape[2] * 2 // LANE)
    quarters = block // LANE
    all_quarters = (packed_ref.shape[1] - segment_rows) // (member_rows * bands)
    for q in range(quarters):
        lanes = slice(q * LANE, (q + 1) * LANE)
        for band in range(bands):
            for j in range(groups):
                source = segment_rows + ((step * quarters + q) * bands + band) * member_rows
                target = (band * groups + j) * member_rows
                weight_ref[target : target + member_rows, lanes] = packed_ref[
                    j, pl.ds(pl.multiple_of(source, 8), member_rows), :
                ]
    amp = amp_ref[...]
    weight = amp * weight_ref[...]
    sigma_ref[...] += jnp.sum((weight * amp).reshape(-1, 8, block), axis=0)
    weight = weight * scale
    x_re = x_re * weight
    x_im = x_im * weight
    coarse = depth // COARSE
    for m in range(templates):
        c0 = chirp_ref[m, 0, coarse:, :]
        s0 = chirp_ref[m, 1, coarse:, :]
        for i in range(coarse):
            span = slice(i * COARSE, (i + 1) * COARSE)
            c1 = chirp_ref[m, 0, i : i + 1, :]
            s1 = chirp_ref[m, 1, i : i + 1, :]
            c = c1 * c0 - s1 * s0
            s = s1 * c0 + c1 * s0
            a, b = x_re[span], x_im[span]
            re_ref[m, span, :] = a * c - b * s
            im_ref[m, span, :] = a * s + b * c


def inverse_kernel(
    block, templates,
    re_ref, im_ref, i1_ref, twist_ref, i2_ref, sigma_ref,
    out_ref,
    c_buf, i1_buf, i2_buf, g_buf,
):
    step = pl.program_id(0)
    inner = re_ref.shape[2]
    depth = re_ref.shape[1]
    half = i2_buf.shape[2]
    i1_coarse = i1_ref.shape[1] - FINE
    i2_coarse = i2_ref.shape[1] - FINE
    twist_coarse = twist_ref.shape[1] - FINE

    @pl.when(step == 0)
    def _():
        for m in range(templates):
            lanes = slice(m * inner, (m + 1) * inner)
            for first in range(0, depth, COARSE):
                rows = slice(first, first + COARSE)
                re = re_ref[m, rows, :]
                im = im_ref[m, rows, :]
                put(c_buf, 0, (rows, lanes), re + im)
                put(c_buf, 1, (rows, lanes), re)
                put(c_buf, 2, (rows, lanes), im)

        @pl.loop(0, i2_coarse)
        def _(outer):
            c, s = product_rows(i2_ref, outer, i2_coarse)
            put_factor(i2_buf, (pl.ds(pl.multiple_of(outer * FINE, FINE), FINE),), c, s)

    per_block = block // FINE

    @pl.loop(0, per_block)
    def _(i):
        rows = (pl.ds(pl.multiple_of(i * FINE, FINE), FINE),)
        c, s = product_rows(i1_ref, step * per_block + i, i1_coarse)
        put_factor(i1_buf, rows, c, s)

    total = jnp.sum(jnp.sum(sigma_ref[...], axis=0, keepdims=True), axis=1, keepdims=True)
    norm = 1.0 / jnp.sqrt(total)
    g_re, g_im = complex_dot(i1_buf, c_buf, NN)
    quarters = block // LANE
    row_stride = templates * (i1_coarse * FINE // LANE)
    for i in range(per_block):
        span = slice(i * FINE, (i + 1) * FINE)
        c, s = product_rows(twist_ref, step * per_block + i, twist_coarse)
        for m in range(templates):
            lanes = slice(m * inner, (m + 1) * inner)
            a, b = g_re[span, lanes], g_im[span, lanes]
            re = a * c - b * s
            im = a * s + b * c
            put(g_buf.at[m], 0, (span,), re + im)
            put(g_buf.at[m], 1, (span,), re)
            put(g_buf.at[m], 2, (span,), im)
    for m in range(templates):
        z_re, z_im = complex_dot(i2_buf, g_buf.at[m], NT)
        size = jnp.sqrt(z_re * z_re + z_im * z_im) * norm
        for q in range(quarters):
            first = (step * quarters + q) * templates + m
            out_ref[pl.ds(first, half, stride=row_stride), :] = size[:, q * LANE : (q + 1) * LANE]


def local(strain, psd_bins, psd_values, chirp_slope, chirp_curve):
    groups = lax.axis_size("tmpl")
    own_part = strain[0]
    half_len = own_part.shape[0]
    sub_len = 2 * half_len
    total_len = sub_len * groups
    inner = sub_len // LANE
    outer = total_len // inner
    depth = 3 * outer // 8
    k_low = total_len // 200
    k_cut = 3 * total_len // 8
    bands = 3 * groups // 8
    templates = chirp_slope.shape[0]
    member_len = psd_bins.shape[1]
    member_rows = member_len // inner
    assert (COARSE * inner) ** 2 % total_len == 0 and 2 * COARSE * inner**2 % total_len == 0
    assert total_len & (total_len - 1) == 0

    tail = shifted(own_part, "tm", 1)
    bins = psd_bins[:bands].reshape(bands, member_rows, inner // LANE, LANE)
    bins = jnp.transpose(bins, (2, 0, 1, 3)).reshape(-1, LANE)
    inv_psd = pl.pallas_call(
        inverse_density,
        out_shape=jax.ShapeDtypeStruct(bins.shape, F32),
        name="inverse_density",
    )(bins, psd_values[0].reshape(-1, LANE))
    packed = jnp.concatenate(
        [tail.reshape(-1, LANE), own_part.reshape(-1, LANE), inv_psd], axis=0
    )
    packed = lax.all_gather(packed, "tmpl", axis=0, tiled=False)

    place = np.arange(outer)
    sample = (place % LANE) * groups + place // LANE
    f1 = base_table(inner, np.arange(inner), inner, -1.0)
    twist1 = base_table(inner, sample, total_len, -1.0)
    f2 = base_table(depth, sample, outer, -1.0)
    i1 = base_table(outer, np.arange(depth), outer, 1.0)
    twist2 = base_table(outer, np.arange(inner), total_len, 1.0)
    i2 = base_table(inner // 2, np.arange(inner), inner, 1.0, inner // 2)

    frequency = (
        jnp.arange(depth, dtype=jnp.int32)[:, None] * inner
        + jnp.arange(inner, dtype=jnp.int32)[None, :]
    )
    ratio = frequency.astype(F32) / k_low
    inside = (frequency >= k_low) & (frequency < k_cut)
    amplitude = jnp.where(inside, jnp.power(jnp.maximum(ratio, 1.0), -7.0 / 6.0), 0.0)

    slope = chirp_slope[:, None, None]
    curve = chirp_curve[:, None, None]
    column = jnp.arange(inner, dtype=jnp.int32)[None, None, :]
    jump = COARSE * inner * jnp.arange(depth // COARSE, dtype=jnp.int32)[None, :, None]
    near = inner * jnp.arange(COARSE, dtype=jnp.int32)[None, :, None] + column
    mask = total_len - 1
    far_phase = slope * jump + curve * ((2 * jump * column) & mask)
    near_phase = slope * near + curve * ((near * near) & mask)
    phase = jnp.concatenate([far_phase, near_phase], axis=1) & mask
    angle = phase.astype(F32) * (TWO_PI / total_len)
    chirp = jnp.stack([jnp.cos(angle), jnp.sin(angle)], axis=1)

    block = 2 * LANE
    whole = lambda *shape: pl.BlockSpec(shape, lambda i: (0,) * len(shape))
    full = lambda array: whole(*array.shape)
    coef_re, coef_im, sigma = pl.pallas_call(
        functools.partial(
            forward_kernel, block, inner, member_rows, templates, 1.0 / math.sqrt(total_len)
        ),
        grid=(inner // block,),
        in_specs=[
            full(packed), full(f1), full(twist1), full(f2),
            pl.BlockSpec((depth, block), lambda i: (0, i)),
            pl.BlockSpec((templates, 2, chirp.shape[2], block), lambda i: (0, 0, 0, i)),
        ],
        out_specs=[
            pl.BlockSpec((templates, depth, block), lambda i: (0, 0, i)),
            pl.BlockSpec((templates, depth, block), lambda i: (0, 0, i)),
            whole(8, block),
        ],
        out_shape=[
            jax.ShapeDtypeStruct((templates, depth, inner), F32),
            jax.ShapeDtypeStruct((templates, depth, inner), F32),
            jax.ShapeDtypeStruct((8, block), F32),
        ],
        scratch_shapes=[
            pltpu.VMEM((2, inner, outer), BF16),
            pltpu.VMEM((2, 2, block, inner), BF16),
            pltpu.VMEM((3, 2, block, outer), BF16),
            pltpu.VMEM((3, 2, depth, outer), BF16),
            pltpu.VMEM((depth, block), F32),
        ],
        compiler_params=pltpu.CompilerParams(vmem_limit_bytes=VMEM_LIMIT),
        name="forward",
    )(packed, f1, twist1, f2, amplitude, chirp)

    half = inner // 2
    rows = half * (outer // LANE) * templates
    flat = pl.pallas_call(
        functools.partial(inverse_kernel, block, templates),
        grid=(outer // block,),
        in_specs=[
            full(coef_re), full(coef_im), full(i1), full(twist2), full(i2), full(sigma),
        ],
        out_specs=whole(rows, LANE),
        out_shape=jax.ShapeDtypeStruct((rows, LANE), F32),
        scratch_shapes=[
            pltpu.VMEM((3, 2, depth, templates * inner), BF16),
            pltpu.VMEM((3, 2, block, depth), BF16),
            pltpu.VMEM((3, 2, half, inner), BF16),
            pltpu.VMEM((templates, 3, 2, block, inner), BF16),
        ],
        compiler_params=pltpu.CompilerParams(vmem_limit_bytes=VMEM_LIMIT),
        name="inverse",
    )(coef_re, coef_im, i1, twist2, i2, sigma)
    result = flat.reshape(-1, templates, LANE)
    return jnp.transpose(result, (1, 0, 2)).reshape(templates, -1)


def solution(mesh):
    placed = (P("tmpl", "tm"), P(None, "tmpl"), P("tm", None), P("tmpl"), P("tmpl"))
    return jax.shard_map(
        local, mesh=mesh, in_specs=placed, out_specs=P("tmpl", "tm"), check_vma=False
    )
```

time: 437 us -> 100 us (0.23); the launches traced: 431 us -> 98.9 us
  local copies, waits for them, and re-layouts: 192 us -> 1.64 us
  matrix products: 139 us -> 0 us
  Pallas kernels: 0 us -> 46.9 us
  other arithmetic: 47.9 us -> 6.96 us
  blocking collectives: 35.1 us -> 0 us
  waiting for transfers between devices: 4.24 us -> 26.8 us
  between operations: 0.81 us -> 13.4 us
  starting transfers between devices: 11.7 us -> 3.2 us
    dot_general x24 -> x0, matrix products: 139 us -> none  [the longest x4 22.6 us: complex_left(): jnp.einsum('qp,...pk->...qk', cos_part, imag_part, precision=HIGHEST)]
    gather x2 -> x0, local copies, waits for them, and re-layouts: 136 us -> none  [local(): inv_psd = 1.0 / jnp.take(psd_values[0], psd_bins[:band_rows])]
    pallas_call x0 -> x3, Pallas kernels: none -> 46.9 us  [the longest x1 22.6 us: local(): pl.pallas_call(functools.partial(inverse_kernel, block, templates), grid=...]
    all_gather x3 -> x0, blocking collectives: 35.1 us -> none  [the longest x1 12.8 us: local(): lax.all_gather(inv_psd, 'tmpl', axis=1, tiled=True)]
    sqrt x3 -> x0, local copies, waits for them, and re-layouts: 30.5 us -> none  [the longest x2 30.5 us: local(): jnp.sqrt(series_re * series_re + series_im * series_im)]
    sub x1 -> x0, other arithmetic: 30 us -> none  [local(): coef_im = white_im * tmpl_re - white_re * tmpl_im]
    all_gather x0 -> x1, waiting for transfers between devices: none -> 26.8 us  [local(): packed = lax.all_gather(packed, 'tmpl', axis=0, tiled=False)]
    pad x2 -> x0, local copies, waits for them, and re-layouts: 13.5 us -> none  [the longest x1 6.95 us: local(): jnp.pad(coef_re, widths)]
  transfers between devices with their start and end apart: 3 -> 2, of which waited for: 1 -> 1; matrix products, arithmetic and copies ran while one was open for 38% -> 7% of each run, Pallas kernels for 0% -> 9%
where the time goes in v1:
time: 100 us; the launch traced here: 98.9 us
  Pallas kernels  46.9 us (47%)
  waiting for transfers between devices  26.8 us (27%)
  between operations  13.4 us (13%)
  other arithmetic  6.96 us (7%)
  starting transfers between devices  3.2 us (3%)
  local copies, waits for them, and re-layouts  1.64 us (2%)
    all_gather x1, waiting for transfers between devices, local(): packed = lax.all_gather(packed, 'tmpl', axis=0, tiled=False)  26.8 us
    pallas_call x1, Pallas kernels, local(): pl.pallas_call(functools.partial(inverse_kernel, block, templates), grid=...  22.6 us
    pallas_call x1, Pallas kernels, local(): pl.pallas_call(functools.partial(forward_kernel, block, inner, member_row...  15.1 us
    pallas_call x1, Pallas kernels, local(): pl.pallas_call(inverse_density, out_shape=jax.ShapeDtypeStruct(bins.shape...  9.1 us
    ppermute x1, starting transfers between devices, shifted(): return lax.ppermute(block, axis, route)  3.19 us
  transfers between devices with their start and end apart: 2, of which 1 were waited for; matrix products, arithmetic and copies ran while one was open for 7% of the time, Pallas kernels for 9%

profile of v1, /device:TPU:9, one launch (start us, length us, event | category | flops | bytes accessed | tf_op | source)
XLA Modules:
  0.0 98.9 jit_solution(15377717338282348851)
XLA Ops:
  6.5 0.0 all-gather.3.cloned.1.call-start
  6.5 3.2 %collective-permute-start = (f32[32768]{0:T(1024)}, f32[32768]{0:T(1024)S(1)}, u32[]{:S(2)}, u32[]{:S(2)}) collective-permute-start(f32[32768]{0:T(1024)} %bitcast.21), channel_id=1, source_target_pairs={{0,8},{8,16},{16,24},{1,9},{9,17},{17,25},{2,10},{10,18},{18,26},{... | collective-permute-start | bytes 393224 | tf_op jit(solution)/shard_map/ppermute | solution.py:26
  9.7 1.0 %reshape.177 = s32[3,16,4,128]{3,2,1,0:T(4,128)S(1)} reshape(s32[3,8192]{1,0:T(4,128)} %bitcast.20) | data formatting | bytes 196608 | tf_op jit(solution)/shard_map/reshape | solution.py:269
  10.7 0.6 copy.12
  11.4 9.1 %inverse_density.1 = f32[192,128]{1,0:T(8,128)} custom-call(s32[192,128]{1,0:T(8,128)} %bitcast.19, f32[64,128]{1,0:T(8,128)} %bitcast.24), custom_call_target="tpu_custom_call" | custom-call | tf_op jit(solution)/shard_map/inverse_density/pallas_call | solution.py:271
  20.5 0.0 collective-permute-done
  20.5 1.7 %pad_maximum_fusion = f32[704,128]{1,0:T(8,128)} fusion(f32[192,128]{1,0:T(8,128)} %inverse_density.1, f32[256,128]{1,0:T(8,128)} %bitcast.22, f32[256,128]{1,0:T(8,128)S(1)} %bitcast.23), kind=kLoop, calls=%fused_computation.5 | loop fusion | flops 180224 | bytes 720896 | tf_op jit(solution)/shard_map/concatenate | solution.py:276
  22.2 0.0 all-gather.3.cloned.1.call-update
  22.3 0.7 broadcast_multiply_fusion
  23.0 0.1 multiply_and_fusion
  23.1 0.1 iota_add_fusion.1
  23.2 0.8 add_bitcast_fusion.1
  23.9 0.7 add_bitcast_fusion
  24.7 0.6 fusion.6
  25.3 0.7 pad_maximum_fusion.1.chirp_ref
  26.0 1.5 %power_select_fusion.amp_ref = f32[384,512]{1,0:T(8,128)} fusion(s32[384]{0:T(512)S(1)} %iota_multiply_fusion), kind=kLoop, calls=%fused_computation | loop fusion | flops 1572864 | bytes 787968 | tf_op jit(solution)/shard_map/jit(_where)/select_n | solution.py:296
  27.5 26.8 %all-gather.3.cloned.1.call-done = f32[5632,128]{1,0:T(8,128)} async-done(((f32[704,128]{1,0:T(8,128)}), f32[5632,128]{1,0:T(8,128)}) %all-gather.3.cloned.1.call-update) | async-done | bytes 2883600 | tf_op jit(solution)/shard_map/all_gather | solution.py:279
  54.3 15.1 %forward.1 = (f32[2,384,512]{2,1,0:T(8,128)}, f32[2,384,512]{2,1,0:T(8,128)}, f32[8,256]{1,0:T(8,128)}) custom-call(f32[8,704,128]{2,1,0:T(8,128)} %bitcast.18, f32[2,48,512]{2,1,0:T(8,128)} %constant.16.clone.f1_ref, f32[2,48,1024]{2,1,0:T(8,128)} %constant.40.clone.twist_ref, f32[2,44,1024]{2,1,0:T(8,128)} %constant.41.clone.f2_ref, ...), custom_call_target="tpu_custom_call" | custom-call | tf_op jit(solution)/shard_map/forward/pallas_call | solution.py:313
  69.5 22.6 %inverse.1 = f32[4096,128]{1,0:T(8,128)} custom-call(f32[2,384,512]{2,1,0:T(8,128)} %get-tuple-element.8.re_ref, f32[2,384,512]{2,1,0:T(8,128)} %get-tuple-element.9.im_ref, f32[2,64,384]{2,1,0:T(8,128)} %constant.42.clone.i1_ref, f32[2,64,512]{2,1,0:T(8,128)} %constant.43.clone.twist_ref, f32[2,40,512]{2,1,0:T(8,128)} %constant.44.clone.i2_ref, ...), custom_call_target="tpu_custom_call" | custom-call | tf_op jit(solution)/shard_map/inverse/pallas_call | solution.py:346
  (4 shorter events, 0.0 us)
Async XLA Ops:
  6.5 47.8 %all-gather.3.cloned.1.call-start = ((), (), s32[]{:S(2)}) async-start(), calls=%async_computation | async-start | bytes 3244032 | tf_op jit(solution)/shard_map/all_gather | solution.py:279
  6.5 14.0 %collective-permute-start = (f32[32768]{0:T(1024)}, f32[32768]{0:T(1024)S(1)}, u32[]{:S(2)}, u32[]{:S(2)}) collective-permute-start(f32[32768]{0:T(1024)} %bitcast.21), channel_id=1, source_target_pairs={{0,8},{8,16},{16,24},{1,9},{9,17},{17,25},{2,10},{10,18},{18,26},{... | collective-permute-start | bytes 393224 | tf_op jit(solution)/shard_map/ppermute | solution.py:26
Sparse Core Ops, SparseCore 0:
  22.4 31.9 all-gather.2

commit v2 on v1

--- a/solution.py
+++ b/solution.py
@@ -74,26 +74,251 @@
     return k1 - k3, k1 + k2
 
 
-def inverse_density(bins_ref, table_ref, out_ref):
-    rows = bins_ref.shape[0]
-    step = next(n for n in (64, 48, 32, 24, 16, 8) if rows % n == 0)
-    for first in range(0, rows, step):
-        bins = bins_ref[first : first + step, :]
-        high = bins // LANE
-        low = bins % LANE
-
-        def body(row, total):
-            line = jnp.broadcast_to(table_ref[pl.ds(row, 1), :], (step, LANE))
-            return jnp.where(
-                high == row,
-                jnp.take_along_axis(line, low, axis=1, mode="promise_in_bounds"),
-                total,
-            )
-
-        picked = lax.fori_loop(
-            0, table_ref.shape[0], body, jnp.ones((step, LANE), F32), unroll=4
+def look_up(bins, table_ref):
+    high = bins // LANE
+    low = bins % LANE
+
+    def body(row, total):
+        lanes = pl.ds(pl.multiple_of(row * LANE, LANE), LANE)
+        line = jnp.broadcast_to(table_ref[:, lanes], bins.shape)
+        return jnp.where(
+            high == row,
+            jnp.take_along_axis(line, low, axis=1, mode="promise_in_bounds"),
+            total,
         )
-        out_ref[first : first + step, :] = 1.0 / picked
+
+    picked = lax.fori_loop(
+        0, table_ref.shape[1] // LANE, body, jnp.ones(bins.shape, F32), unroll=4
+    )
+    return 1.0 / picked
+
+
+def density_rows(bins_ref, ordered_ref, bands, inner):
+    member_rows = bins_ref.shape[1] // inner
+    for q in range(inner // LANE):
+        for band in range(bands):
+            for row in range(member_rows):
+                start = row * inner + q * LANE
+                target = (q * bands + band) * member_rows + row
+                ordered_ref[target : target + 1, :] = bins_ref[
+                    band : band + 1, start : start + LANE
+                ]
+
+
+def density_kernel(bands, inner, bins_ref, table_ref, out_ref, ordered_ref):
+    density_rows(bins_ref, ordered_ref, bands, inner)
+    out_ref[...] = look_up(ordered_ref[...], table_ref)
+
+
+def amplitude_rows(first, shape, total_len):
+    k_low = total_len // 200
+    k_cut = 3 * total_len // 8
+    row = first + lax.broadcasted_iota(jnp.int32, shape, 0)
+    frequency = row * shape[1] + lax.broadcasted_iota(jnp.int32, shape, 1)
+    ratio = jnp.maximum(frequency.astype(F32) / k_low, 1.0)
+    inside = (frequency >= k_low) & (frequency < k_cut)
+    return jnp.where(inside, jnp.exp(jnp.log(ratio) * (-7.0 / 6.0)), 0.0)
+
+
+def template_rows(slope_ref, curve_ref, chirp_ref, m, total_len):
+    inner = chirp_ref.shape[3]
+    coarse = chirp_ref.shape[2] - COARSE
+    for first in range(0, coarse + COARSE, 8):
+        slope = slope_ref[m]
+        curve = curve_ref[m]
+        if first < coarse:
+            row = first
+            jump = COARSE * inner
+        else:
+            row = first - coarse
+            jump = 0
+        shape = (8, inner)
+        index = row + lax.broadcasted_iota(jnp.int32, shape, 0)
+        column = lax.broadcasted_iota(jnp.int32, shape, 1)
+        mask = total_len - 1
+        if jump:
+            far = jump * index
+            phase = slope * far + curve * ((2 * far * column) & mask)
+        else:
+            near = inner * index + column
+            phase = slope * near + curve * ((near * near) & mask)
+        angle = (phase & mask).astype(F32) * (TWO_PI / total_len)
+        chirp_ref[m, 0, first : first + 8, :] = jnp.cos(angle)
+        chirp_ref[m, 1, first : first + 8, :] = jnp.sin(angle)
+
+
+def amplitude_table(amp_ref, total_len):
+    depth, inner = amp_ref.shape
+
+    @pl.loop(0, depth // 8)
+    def _(i):
+        first = pl.multiple_of(i * 8, 8)
+        amp_ref[pl.ds(first, 8), :] = amplitude_rows(first, (8, inner), total_len)
+
+
+def table_kernel(total_len, slope_ref, curve_ref, chirp_ref, amp_ref):
+    for m in range(chirp_ref.shape[0]):
+        template_rows(slope_ref, curve_ref, chirp_ref, m, total_len)
+    amplitude_table(amp_ref, total_len)
+
+
+def gather_kernel(
+    bands, inner, total_len,
+    own_ref, bins_ref, table_ref, slope_ref, curve_ref,
+    out_ref, chirp_ref, amp_ref,
+    ordered_ref, send_sem, recv_sem, tail_send, tail_recv,
+):
+    tm = lax.axis_index("tm")
+    me = lax.axis_index("tmpl")
+    count = lax.axis_size("tm")
+    half = own_ref.shape[0]
+    extra = ordered_ref.shape[0]
+
+    def peer(distance):
+        low = me % (2 * distance)
+        return me - low + (low + distance) % (2 * distance)
+
+    core = peer(1)
+    side = peer(2)
+    front = peer(4)
+    side_front = side + front - me
+    spans = ((half, half), (0, half), (2 * half, extra))
+
+    barrier = pltpu.get_barrier_semaphore()
+    for other in (core, side, front):
+        pl.semaphore_signal(
+            barrier, inc=1, device_id={"tmpl": other}, device_id_type=pl.DeviceIdType.MESH
+        )
+
+    for other in ((tm + 1) % count, (tm + count - 1) % count):
+        pl.semaphore_signal(
+            barrier, inc=1, device_id={"tm": other}, device_id_type=pl.DeviceIdType.MESH
+        )
+    pl.semaphore_wait(barrier, 5)
+
+    def copy(part, kind, slot, piece, target, source=None):
+        first, rows = spans[part]
+        if piece is not None:
+            rows = rows // 2
+            first = first + piece * rows
+        view = out_ref.at[slot, pl.ds(first, rows), :]
+        return pltpu.make_async_remote_copy(
+            src_ref=view if source is None else source,
+            dst_ref=view,
+            send_sem=send_sem.at[part, kind],
+            recv_sem=recv_sem.at[part, kind],
+            device_id={"tmpl": target},
+            device_id_type=pl.DeviceIdType.MESH,
+        )
+
+    def send(part, kind, source=None):
+        slot, piece, target = (
+            (me, None, core), (me, None, side), (me, None, front),
+            (side, None, core), (front, None, core),
+            (side, 0, front), (front, 1, side),
+            (side_front, 0, core), (side_front, 1, core),
+        )[kind]
+        return copy(part, kind, slot, piece, target, source if kind < 3 else None)
+
+    def first_stage(part, source=None):
+        send(part, 1, source).start()
+        send(part, 2, source).start()
+        send(part, 0, source).start()
+
+    def second_stage(part):
+        copy(part, 1, side, None, side).wait_recv()
+        send(part, 5).start()
+        copy(part, 2, front, None, front).wait_recv()
+        send(part, 6).start()
+        send(part, 3).start()
+        send(part, 4).start()
+
+    def third_stage(part):
+        copy(part, 5, side_front, 0, front).wait_recv()
+        send(part, 7).start()
+        copy(part, 6, side_front, 1, side).wait_recv()
+        send(part, 8).start()
+
+    def last_stage(part, source=None):
+        other = core + side - me
+        across = core + front - me
+        corner = core + side_front - me
+        copy(part, 0, core, None, core).wait_recv()
+        copy(part, 3, other, None, core).wait_recv()
+        copy(part, 4, across, None, core).wait_recv()
+        copy(part, 7, corner, 0, core).wait_recv()
+        copy(part, 8, corner, 1, core).wait_recv()
+        for kind in range(9):
+            send(part, kind, source).wait_send()
+
+    tail_view = out_ref.at[me, pl.ds(0, half), :]
+    tail = pltpu.make_async_remote_copy(
+        src_ref=own_ref,
+        dst_ref=tail_view,
+        send_sem=tail_send,
+        recv_sem=tail_recv,
+        device_id={"tm": (tm + 1) % count},
+        device_id_type=pl.DeviceIdType.MESH,
+    )
+
+    @pl.when(tm < count - 1)
+    def _():
+        tail.start()
+
+    first_stage(0, own_ref)
+    out_ref[me, half : 2 * half, :] = own_ref[...]
+    density_rows(bins_ref, ordered_ref, bands, inner)
+    third = extra // 3
+
+    def densities(i):
+        rows = slice(i * third, (i + 1) * third)
+        out_ref[me, 2 * half + i * third : 2 * half + (i + 1) * third, :] = look_up(
+            ordered_ref[rows, :], table_ref
+        )
+
+    @pl.when(tm == 0)
+    def _():
+        for slot in range(out_ref.shape[0]):
+            out_ref[slot, :half, :] = jnp.zeros((half, LANE), F32)
+
+    @pl.when(tm > 0)
+    def _():
+        tail.wait_recv()
+        first_stage(1)
+
+    densities(0)
+    second_stage(0)
+    densities(1)
+    densities(2)
+    first_stage(2)
+    third_stage(0)
+
+    @pl.when(tm > 0)
+    def _():
+        second_stage(1)
+
+    template_rows(slope_ref, curve_ref, chirp_ref, 0, total_len)
+
+    @pl.when(tm > 0)
+    def _():
+        third_stage(1)
+
+    second_stage(2)
+    for m in range(1, chirp_ref.shape[0]):
+        template_rows(slope_ref, curve_ref, chirp_ref, m, total_len)
+    third_stage(2)
+    amplitude_table(amp_ref, total_len)
+    last_stage(0, own_ref)
+
+    @pl.when(tm > 0)
+    def _():
+        last_stage(1)
+
+    last_stage(2)
+
+    @pl.when(tm < count - 1)
+    def _():
+        tail.wait_send()
 
 
 def forward_kernel(
@@ -265,18 +490,48 @@
     assert (COARSE * inner) ** 2 % total_len == 0 and 2 * COARSE * inner**2 % total_len == 0
     assert total_len & (total_len - 1) == 0
 
-    tail = shifted(own_part, "tm", 1)
-    bins = psd_bins[:bands].reshape(bands, member_rows, inner // LANE, LANE)
-    bins = jnp.transpose(bins, (2, 0, 1, 3)).reshape(-1, LANE)
-    inv_psd = pl.pallas_call(
-        inverse_density,
-        out_shape=jax.ShapeDtypeStruct(bins.shape, F32),
-        name="inverse_density",
-    )(bins, psd_values[0].reshape(-1, LANE))
-    packed = jnp.concatenate(
-        [tail.reshape(-1, LANE), own_part.reshape(-1, LANE), inv_psd], axis=0
-    )
-    packed = lax.all_gather(packed, "tmpl", axis=0, tiled=False)
+    extra = bands * member_len // LANE
+    table_shapes = [
+        jax.ShapeDtypeStruct((templates, 2, depth // COARSE + COARSE, inner), F32),
+        jax.ShapeDtypeStruct((depth, inner), F32),
+    ]
+    vmem = pl.BlockSpec(memory_space=pltpu.VMEM)
+    smem = pl.BlockSpec(memory_space=pltpu.SMEM)
+    own_rows = own_part.reshape(-1, LANE)
+    rows = 2 * own_rows.shape[0] + extra
+    if groups == 8:
+        packed, chirp, amplitude = pl.pallas_call(
+            functools.partial(gather_kernel, bands, inner, total_len),
+            in_specs=[vmem, vmem, vmem, smem, smem],
+            out_specs=[vmem, vmem, vmem],
+            out_shape=[jax.ShapeDtypeStruct((groups, rows, LANE), F32)] + table_shapes,
+            scratch_shapes=[
+                pltpu.VMEM((extra, LANE), jnp.int32),
+                pltpu.SemaphoreType.DMA((3, 9)),
+                pltpu.SemaphoreType.DMA((3, 9)),
+                pltpu.SemaphoreType.DMA,
+                pltpu.SemaphoreType.DMA,
+            ],
+            compiler_params=pltpu.CompilerParams(collective_id=0, has_side_effects=True),
+            name="gather",
+        )(own_rows, psd_bins, psd_values, chirp_slope, chirp_curve)
+    else:
+        tail = shifted(own_part, "tm", 1).reshape(-1, LANE)
+        inv_psd = pl.pallas_call(
+            functools.partial(density_kernel, bands, inner),
+            out_shape=jax.ShapeDtypeStruct((extra, LANE), F32),
+            scratch_shapes=[pltpu.VMEM((extra, LANE), jnp.int32)],
+            name="density",
+        )(psd_bins, psd_values)
+        packed = lax.all_gather(
+            jnp.concatenate([tail, own_rows, inv_psd], axis=0), "tmpl", axis=0, tiled=False
+        )
+        chirp, amplitude = pl.pallas_call(
+            functools.partial(table_kernel, total_len),
+            in_specs=[smem, smem],
+            out_shape=table_shapes,
+            name="tables",
+        )(chirp_slope, chirp_curve)
 
     place = np.arange(outer)
     sample = (place % LANE) * groups + place // LANE
@@ -286,26 +541,6 @@
     i1 = base_table(outer, np.arange(depth), outer, 1.0)
     twist2 = base_table(outer, np.arange(inner), total_len, 1.0)
     i2 = base_table(inner // 2, np.arange(inner), inner, 1.0, inner // 2)
-
-    frequency = (
-        jnp.arange(depth, dtype=jnp.int32)[:, None] * inner
-        + jnp.arange(inner, dtype=jnp.int32)[None, :]
-    )
-    ratio = frequency.astype(F32) / k_low
-    inside = (frequency >= k_low) & (frequency < k_cut)
-    amplitude = jnp.where(inside, jnp.power(jnp.maximum(ratio, 1.0), -7.0 / 6.0), 0.0)
-
-    slope = chirp_slope[:, None, None]
-    curve = chirp_curve[:, None, None]
-    column = jnp.arange(inner, dtype=jnp.int32)[None, None, :]
-    jump = COARSE * inner * jnp.arange(depth // COARSE, dtype=jnp.int32)[None, :, None]
-    near = inner * jnp.arange(COARSE, dtype=jnp.int32)[None, :, None] + column
-    mask = total_len - 1
-    far_phase = slope * jump + curve * ((2 * jump * column) & mask)
-    near_phase = slope * near + curve * ((near * near) & mask)
-    phase = jnp.concatenate([far_phase, near_phase], axis=1) & mask
-    angle = phase.astype(F32) * (TWO_PI / total_len)
-    chirp = jnp.stack([jnp.cos(angle), jnp.sin(angle)], axis=1)
 
     block = 2 * LANE
     whole = lambda *shape: pl.BlockSpec(shape, lambda i: (0,) * len(shape))

time: 100 us -> 66.3 us (0.66)
  waiting for transfers between devices: 26.8 us -> 0 us
  Pallas kernels: 46.9 us -> 66.2 us
  between operations: 13.4 us -> 0.01 us
  other arithmetic: 6.96 us -> 0 us
  starting transfers between devices: 3.2 us -> 0 us
  local copies, waits for them, and re-layouts: 1.64 us -> 0 us
    all_gather x1 -> x0, waiting for transfers between devices: 26.8 us -> none  [local(): packed = lax.all_gather(packed, 'tmpl', axis=0, tiled=False)]
    pallas_call x1, Pallas kernels: 9.1 us -> 28.4 us  [local(): pl.pallas_call(functools.partial(gather_kernel, bands, inner, total_len),...]
    concatenate x3 -> x0, other arithmetic: 3.22 us -> none  [the longest x1 1.74 us: local(): jnp.concatenate([tail.reshape(-1, LANE), own_part.reshape(-1, LANE), inv_...]
    ppermute x1 -> x0, starting transfers between devices: 3.19 us -> none  [shifted(): return lax.ppermute(block, axis, route)]
    reshape x2 -> x0, local copies, waits for them, and re-layouts: 1.64 us -> none  [local(): bins = psd_bins[:bands].reshape(bands, member_rows, inner // LANE, LANE)]
    select_n x1 -> x0, other arithmetic: 1.51 us -> none  [local(): jnp.where(inside, jnp.power(jnp.maximum(ratio, 1.0), -7.0 / 6.0), 0.0)]
  transfers between devices with their start and end apart: 2 -> 0, of which waited for: 1 -> 0; matrix products, arithmetic and copies ran while one was open for 7% -> 0% of each run, Pallas kernels for 9% -> 0%
where the time goes in v2:
time: 66.3 us; the launch traced here: 66.2 us
  Pallas kernels  66.2 us (100%)
    pallas_call x1, Pallas kernels, local(): pl.pallas_call(functools.partial(gather_kernel, bands, inner, total_len),...  28.4 us
    pallas_call x1, Pallas kernels, local(): pl.pallas_call(functools.partial(inverse_kernel, block, templates), grid=...  22.6 us
    pallas_call x1, Pallas kernels, local(): pl.pallas_call(functools.partial(forward_kernel, block, inner, member_row...  15.2 us

profile of v2, /device:TPU:9, one launch (start us, length us, event | category | flops | bytes accessed | tf_op | source)
XLA Modules:
  0.0 66.2 jit_solution(17343478269569575471)
XLA Ops:
  0.0 28.4 %gather.1 = (f32[8,704,128]{2,1,0:T(8,128)}, f32[2,2,40,512]{3,2,1,0:T(8,128)}, f32[384,512]{1,0:T(8,128)}) custom-call(f32[256,128]{1,0:T(8,128)} %bitcast.6, s32[4,8192]{1,0:T(4,128)} %bins_ref.1, f32[1,8192]{1,0:T(1,128)} %table_ref.1, s32[2]{0:T(128)} %slope_ref.1, s32[2]{0:T(128)} %curve_ref.1), custom_call_target="tpu_custom_call" | custom-call | tf_op jit(solution)/shard_map/gather/pallas_call | solution.py:503
  28.4 15.2 %forward.1 = (f32[2,384,512]{2,1,0:T(8,128)}, f32[2,384,512]{2,1,0:T(8,128)}, f32[8,256]{1,0:T(8,128)}) custom-call(f32[8,704,128]{2,1,0:T(8,128)} %get-tuple-element.11.packed_ref, f32[2,48,512]{2,1,0:T(8,128)} %constant.12.clone.f1_ref, f32[2,48,1024]{2,1,0:T(8,128)} %constant.13.clone.twist_ref, f32[2,44,1024]{2,1,0:T(8,128)} %constant.14.clone.f2_ref, ...), custom_call_target="tpu_custom_call" | custom-call | tf_op jit(solution)/shard_map/forward/pallas_call | solution.py:548
  43.6 22.6 %inverse.1 = f32[4096,128]{1,0:T(8,128)} custom-call(f32[2,384,512]{2,1,0:T(8,128)} %get-tuple-element.14.re_ref, f32[2,384,512]{2,1,0:T(8,128)} %get-tuple-element.15.im_ref, f32[2,64,384]{2,1,0:T(8,128)} %constant.15.clone.i1_ref, f32[2,64,512]{2,1,0:T(8,128)} %constant.16.clone.twist_ref, f32[2,40,512]{2,1,0:T(8,128)} %constant.17.clone.i2_ref, ...), custom_call_target="tpu_custom_call" | custom-call | tf_op jit(solution)/shard_map/inverse/pallas_call | solution.py:581

commit v3 on v2

--- a/solution.py
+++ b/solution.py
@@ -60,11 +60,15 @@
     put(ref, 2, index, re + im)
 
 
+def split_dot(a_high, a_low, b_high, b_low, dims):
+    ((a_axis,), (b_axis,)), _ = dims
+    a = jnp.concatenate([a_high, a_low, a_high], axis=a_axis)
+    b = jnp.concatenate([b_low, b_high, b_high], axis=b_axis)
+    return lax.dot_general(a, b, dims, preferred_element_type=F32)
+
+
 def dot3(a, b, slot, dims):
-    def one(i, j):
-        return lax.dot_general(a[slot, i], b[slot, j], dims, preferred_element_type=F32)
-
-    return one(0, 0) + (one(0, 1) + one(1, 0))
+    return split_dot(a[slot, 0], a[slot, 1], b[slot, 0], b[slot, 1], dims)
 
 
 def complex_dot(a, b, dims):
@@ -358,10 +362,7 @@
         put(f1_buf, 1, rows, s)
 
     def real_dot(slot):
-        def one(i, j):
-            return lax.dot_general(f1_buf[slot, i], x_ref[j], NN, preferred_element_type=F32)
-
-        return one(0, 0) + (one(0, 1) + one(1, 0))
+        return split_dot(f1_buf[slot, 0], f1_buf[slot, 1], x_ref[0], x_ref[1], NN)
 
     y_re = real_dot(0)
     y_im = real_dot(1)

time: 66.3 us -> 63.9 us (0.964)
  Pallas kernels: 66.2 us -> 63.7 us
    pallas_call x1, Pallas kernels: 22.6 us -> 20.1 us  [local(): pl.pallas_call(functools.partial(inverse_kernel, block, templates), grid=...]
where the time goes in v3:
time: 63.9 us; the launch traced here: 63.7 us
  Pallas kernels  63.7 us (100%)
    pallas_call x1, Pallas kernels, local(): pl.pallas_call(functools.partial(gather_kernel, bands, inner, total_len),...  28.4 us
    pallas_call x1, Pallas kernels, local(): pl.pallas_call(functools.partial(inverse_kernel, block, templates), grid=...  20.1 us
    pallas_call x1, Pallas kernels, local(): pl.pallas_call(functools.partial(forward_kernel, block, inner, member_row...  15.2 us

profile of v3, /device:TPU:9, one launch (start us, length us, event | category | flops | bytes accessed | tf_op | source)
XLA Modules:
  0.0 63.7 jit_solution(14424631901911436268)
XLA Ops:
  0.0 28.4 %gather.1 = (f32[8,704,128]{2,1,0:T(8,128)}, f32[2,2,40,512]{3,2,1,0:T(8,128)}, f32[384,512]{1,0:T(8,128)}) custom-call(f32[256,128]{1,0:T(8,128)} %bitcast.6, s32[4,8192]{1,0:T(4,128)} %bins_ref.1, f32[1,8192]{1,0:T(1,128)} %table_ref.1, s32[2]{0:T(128)} %slope_ref.1, s32[2]{0:T(128)} %curve_ref.1), custom_call_target="tpu_custom_call" | custom-call | tf_op jit(solution)/shard_map/gather/pallas_call | solution.py:504
  28.4 15.2 %forward.1 = (f32[2,384,512]{2,1,0:T(8,128)}, f32[2,384,512]{2,1,0:T(8,128)}, f32[8,256]{1,0:T(8,128)}) custom-call(f32[8,704,128]{2,1,0:T(8,128)} %get-tuple-element.11.packed_ref, f32[2,48,512]{2,1,0:T(8,128)} %constant.12.clone.f1_ref, f32[2,48,1024]{2,1,0:T(8,128)} %constant.13.clone.twist_ref, f32[2,44,1024]{2,1,0:T(8,128)} %constant.14.clone.f2_ref, ...), custom_call_target="tpu_custom_call" | custom-call | tf_op jit(solution)/shard_map/forward/pallas_call | solution.py:549
  43.6 20.1 %inverse.1 = f32[4096,128]{1,0:T(8,128)} custom-call(f32[2,384,512]{2,1,0:T(8,128)} %get-tuple-element.14.re_ref, f32[2,384,512]{2,1,0:T(8,128)} %get-tuple-element.15.im_ref, f32[2,64,384]{2,1,0:T(8,128)} %constant.15.clone.i1_ref, f32[2,64,512]{2,1,0:T(8,128)} %constant.16.clone.twist_ref, f32[2,40,512]{2,1,0:T(8,128)} %constant.17.clone.i2_ref, ...), custom_call_target="tpu_custom_call" | custom-call | tf_op jit(solution)/shard_map/inverse/pallas_call | solution.py:582
